TPU v7x, 32 devices: a whole 2x2x4 slice. The times are simulated.
32 devices in a mesh: prow: 4 (over y, x), pcol: 8 (over z, core).
Axes of the slice: x: 2, y: 2, z: 4, core: 2. Of those that a mesh axis runs over, the one named last changes fastest.
Arguments:
- matrix: float32 [12288, 12288], P('prow', 'pcol'), may hold values from -6 to 6, as said below
- reflectors: float32 [12288, 512], P('prow'), may hold values from -0.0546875 to 0.0546875
- factors: float32 [2, 256, 256], replicated, may hold values from -0.25 to 2, as said below
Outputs:
- updated: float32 [12288, 12288], P('prow', 'pcol')
Inputs may be any that keep to these rules, and one draw needn't show every extreme that they name: `matrix`: symmetric: entry (i, j) equals entry (j, i). `factors`: each of the 2 blocks is upper triangular with diagonal entries between 1 and 2.
All inputs are finite; a program needn't handle non-finite values.
Results may differ from a plain program's by a relative error of at most 0.0001.
Values sent between devices are 32-bit elements; how exact they have to be, the bound alone decides.
No kernel may reach another device: no remote copies, remote signals or barrier semaphores. Data moves between devices by JAX's collectives and lax.ppermute only.
A program may use at most 128 MiB of HBM per device.

v0:
```python
import functools

import jax
import jax.numpy as jnp
from jax import lax
from jax.experimental import pallas as pl
from jax.experimental.pallas import tpu as pltpu
from jax.sharding import PartitionSpec as P


AXES = ("prow", "pcol")


BF16 = jnp.bfloat16
F32 = jnp.float32
VMEM_LIMIT = 56 << 20


def contract(left, right, left_dim, right_dim, precision=None):
    return lax.dot_general(
        left,
        right,
        (((left_dim,), (right_dim,)), ((), ())),
        precision=precision,
        preferred_element_type=F32,
    )


def halves(value):
    high = value.astype(BF16)
    return high, (value - high.astype(F32)).astype(BF16)


def contract_split(left, right, left_dim, right_dim):
    left_high, left_low = left
    right_high, right_low = right
    return (
        contract(left_high, right_high, left_dim, right_dim)
        + contract(left_low, right_high, left_dim, right_dim)
        + contract(left_high, right_low, left_dim, right_dim)
    )


def params():
    return pltpu.CompilerParams(vmem_limit_bytes=VMEM_LIMIT)


def pair_kernel(slots_ref, vectors_ref, matrix_ref, *refs):
    outs, (high_ref, low_ref) = refs[:-2], refs[-2:]
    width = outs[0].shape[1]

    @pl.when(pl.program_id(0) == 0)
    def _():
        high, low = halves(vectors_ref[...])
        high_ref[...] = high
        low_ref[...] = low

    value = contract_split(halves(matrix_ref[...]), (high_ref[...], low_ref[...]), 0, 0)

    def store(item):
        outs[2 * item][...] = value[:, :width]
        outs[2 * item + 1][...] = value[:, width:]

    for item in range(len(outs) // 2):
        pl.when(pl.program_id(0) == item)(lambda item=item: store(item))


def pair_sums(matrix, reflectors, width, slots, piece):
    rows = matrix.shape[0]
    items = slots.shape[0]
    out = pl.BlockSpec((piece, width), lambda i, s: (0, 0))
    shape = jax.ShapeDtypeStruct((piece, width), F32)
    return pl.pallas_call(
        pair_kernel,
        grid_spec=pltpu.PrefetchScalarGridSpec(
            num_scalar_prefetch=1,
            grid=(items,),
            in_specs=[
                pl.BlockSpec(
                    (rows, 2 * width), lambda i, s: (0, 0), pipeline_mode=pl.Buffered(1)
                ),
                pl.BlockSpec((rows, piece), lambda i, s: (0, s[i])),
            ],
            out_specs=(out,) * (2 * items),
            scratch_shapes=[pltpu.VMEM((rows, 2 * width), BF16)] * 2,
        ),
        out_shape=(shape,) * (2 * items),
        compiler_params=params(),
    )(slots, reflectors, matrix)


def cross_kernel(core_ref, first_ref, second_ref, out_ref):
    out_ref[...] = contract_split(halves(first_ref[...]), halves(second_ref[...]), 0, 0)


def cross_part(core, reflectors, width):
    rows = reflectors.shape[0]
    half = width // 2
    return pl.pallas_call(
        cross_kernel,
        grid_spec=pltpu.PrefetchScalarGridSpec(
            num_scalar_prefetch=1,
            grid=(1,),
            in_specs=[
                pl.BlockSpec((rows, half), lambda i, c: (0, c[0])),
                pl.BlockSpec((rows, width), lambda i, c: (0, 1)),
            ],
            out_specs=pl.BlockSpec((half, width), lambda i, c: (0, 0)),
        ),
        out_shape=jax.ShapeDtypeStruct((half, width), F32),
        compiler_params=params(),
    )(core, reflectors, reflectors)


def gram_kernel(sums_a_ref, sums_b_ref, vectors_ref, out_ref):
    width = sums_a_ref.shape[1]
    first = halves(vectors_ref[:, :width])
    second = halves(vectors_ref[:, width:])
    sums_a = halves(sums_a_ref[...])
    sums_b = halves(sums_b_ref[...])
    out_ref[:width, :] = contract_split(first, sums_a, 0, 0)
    out_ref[width : 2 * width, :] = contract_split(first, sums_b, 0, 0)
    out_ref[2 * width :, :] = contract_split(second, sums_b, 0, 0)


def grams(sums_a, sums_b, vectors):
    width = sums_a.shape[1]
    return pl.pallas_call(
        gram_kernel,
        out_shape=jax.ShapeDtypeStruct((3 * width, width), F32),
        compiler_params=params(),
    )(sums_a, sums_b, vectors)


def exact(left, right, left_dim=1, right_dim=0):
    return contract(left, right, left_dim, right_dim, lax.Precision.HIGHEST)


def mixing(first, second, c12):
    t1_c = exact(first, c12)
    top = jnp.concatenate([first, -exact(t1_c, second)], axis=1)
    bottom = jnp.concatenate([jnp.zeros_like(first), second], axis=1)
    return jnp.concatenate([top, bottom])


def coupling(first, second, c12, g11, g12, g22):
    t1_c = exact(first, c12)
    m1 = exact(first, exact(g11, first), 0, 0)
    half_m1_c = 0.5 * exact(m1, c12)
    lead = half_m1_c - (exact(first, g12, 0, 0) - 0.5 * exact(m1, c12, 0, 0))
    inner = g22 - exact(g12, t1_c, 0, 0) + exact(c12, lead, 0, 0)
    m2 = exact(second, exact(inner, second), 0, 0)
    cross = exact(lead, second)
    top = jnp.concatenate([-0.5 * (m1 + m1.T), cross], axis=1)
    bottom = jnp.concatenate([cross.T, -0.5 * (m2 + m2.T)], axis=1)
    return jnp.concatenate([top, bottom])


def finish_kernel(factors_ref, c12_ref, gram_ref, lead_ref, high_ref, low_ref, *refs):
    out_high, out_low, k_high, k_low = refs
    width = factors_ref.shape[1]

    @pl.when(pl.program_id(0) == 0)
    def _():
        k = coupling(
            factors_ref[0],
            factors_ref[1],
            c12_ref[...],
            gram_ref[:width, :],
            gram_ref[width : 2 * width, :],
            gram_ref[2 * width :, :],
        )
        k_high[...], k_low[...] = halves(k)

    value = lead_ref[...] + contract_split(
        (high_ref[...], low_ref[...]), (k_high[...], k_low[...]), 1, 0
    )
    out_high[...], out_low[...] = halves(value)


def finish_factors(factors, c12, gram, lead, high, low, piece):
    cols, depth = lead.shape
    width = factors.shape[1]
    tile = pl.BlockSpec((piece, depth), lambda j: (j, 0))
    shape = jax.ShapeDtypeStruct((cols, depth), BF16)
    return pl.pallas_call(
        finish_kernel,
        grid=(cols // piece,),
        in_specs=[
            pl.BlockSpec((2, width, width), lambda j: (0, 0, 0)),
            pl.BlockSpec((width, width), lambda j: (0, 0)),
            pl.BlockSpec((3 * width, width), lambda j: (0, 0)),
            tile,
            tile,
            tile,
        ],
        out_specs=(tile, tile),
        out_shape=(shape, shape),
        scratch_shapes=[pltpu.VMEM((depth, depth), BF16)] * 2,
        compiler_params=params(),
    )(factors, c12, gram, lead, high, low)


def slot_pieces(refs):
    own, near_a, near_b, far_a, far_b = refs
    return (
        own[...],
        jnp.concatenate([near_a[...], far_b[0]], axis=1),
        jnp.concatenate([far_a[0], near_b[...]], axis=1),
        jnp.concatenate([far_a[1], far_b[1]], axis=1),
    )


def rows_of(row_ref, slot, piece):
    return pl.ds(pl.multiple_of((row_ref[0] ^ slot) * piece, piece), piece)


def vector_column_kernel(row_ref, factors_ref, c12_ref, *refs):
    right_high, right_low, vector_high, vector_low, x_high, x_low = refs[5:]
    piece = refs[0].shape[0]
    x = halves(mixing(factors_ref[0], factors_ref[1], c12_ref[...]))
    x_high[...], x_low[...] = x
    for slot, value in enumerate(slot_pieces(refs[:5])):
        vectors = halves(value)
        at = rows_of(row_ref, slot, piece)
        right_high[at, :], right_low[at, :] = halves(contract_split(vectors, x, 1, 1))
        vector_high[at, :], vector_low[at, :] = vectors


def sum_column_kernel(row_ref, x_high, x_low, *refs):
    piece = refs[0].shape[0]
    x = (x_high[...], x_low[...])
    for slot, value in enumerate(slot_pieces(refs[:5])):
        refs[5][rows_of(row_ref, slot, piece), :] = contract_split(halves(value), x, 1, 0)


def column_call(kernel, shapes, row, *args):
    whole = pl.BlockSpec(memory_space=pltpu.VMEM)
    return pl.pallas_call(
        kernel,
        in_specs=[pl.BlockSpec(memory_space=pltpu.SMEM)] + [whole] * len(args),
        out_specs=(whole,) * len(shapes),
        out_shape=tuple(jax.ShapeDtypeStruct(*shape) for shape in shapes),
        compiler_params=params(),
    )(row, *args)


def vector_update_kernel(matrix_ref, vectors_ref, high_ref, low_ref, out_ref):
    out_ref[...] = matrix_ref[...] - contract_split(
        halves(vectors_ref[...]), (high_ref[...], low_ref[...]), 1, 1
    )


def vector_update(matrix, reflectors, high, low, piece):
    rows, cols = matrix.shape
    depth = reflectors.shape[1]
    resident = pl.BlockSpec((cols, depth), lambda j: (0, 0), pipeline_mode=pl.Buffered(1))
    return pl.pallas_call(
        vector_update_kernel,
        grid=(rows // piece,),
        in_specs=[
            pl.BlockSpec((piece, cols), lambda j: (j, 0)),
            pl.BlockSpec((piece, depth), lambda j: (j, 0)),
            resident,
            resident,
        ],
        out_specs=pl.BlockSpec((piece, cols), lambda j: (j, 0)),
        out_shape=jax.ShapeDtypeStruct((rows, cols), F32),
        compiler_params=params(),
    )(matrix, reflectors, high, low)


def sum_update_kernel(block_ref, matrix_ref, high_ref, low_ref, *refs, sources):
    out_ref = refs[-1]

    def update(source):
        out_ref[...] = matrix_ref[...] - contract_split(
            halves(source[...]), (high_ref[...], low_ref[...]), 1, 1
        )

    for index in range(sources):
        pl.when(pl.program_id(0) == index)(lambda index=index: update(refs[index]))


def sum_update(blocks, matrix, high, low, sources):
    rows, cols = matrix.shape
    piece, depth = sources[0].shape
    count = len(sources)
    resident = pl.BlockSpec((cols, depth), lambda j, b: (0, 0), pipeline_mode=pl.Buffered(1))
    whole = pl.BlockSpec((piece, depth), lambda j, b: (0, 0), pipeline_mode=pl.Buffered(1))
    tile = pl.BlockSpec((piece, cols), lambda j, b: (b[j], 0))
    return pl.pallas_call(
        functools.partial(sum_update_kernel, sources=count),
        grid_spec=pltpu.PrefetchScalarGridSpec(
            num_scalar_prefetch=1,
            grid=(count,),
            in_specs=[tile, resident, resident]
            + [whole] * count,
            out_specs=tile,
        ),
        out_shape=jax.ShapeDtypeStruct((rows, cols), F32),
        input_output_aliases={1: 0},
        compiler_params=params(),
    )(blocks, matrix, high, low, *sources)


def quad_body(matrix, reflectors, factors):
    size = lax.axis_size("prow")
    width = factors.shape[1]
    _, cols = matrix.shape
    piece = cols // size
    row = lax.axis_index("prow")
    col = lax.axis_index("pcol")
    core = col % 2
    level = col // 2

    def send(value, target):
        pairs = []
        for r in range(size):
            for z in range(size):
                for k in range(2):
                    to = target(r, z, k)
                    if to is not None:
                        source = (r * size + z) * 2 + k
                        pairs.append((source, (to[0] * size + to[1]) * 2 + to[2]))
        return lax.ppermute(value, AXES, pairs)

    def across(step):
        return lambda r, z, k: (r ^ step, z, k)

    def sibling(value):
        return send(value, lambda r, z, k: (r, z, k ^ 1))

    sub = piece // size

    def quarter(index):
        start = core * cols + index * piece + level * sub
        return lax.dynamic_slice_in_dim(reflectors, start, sub, 0)

    def pick(stack, index):
        return lax.dynamic_index_in_dim(stack, index, 0, keepdims=False)

    def pair(slots):
        return pair_sums(
            matrix, reflectors, width, jnp.array(slots, jnp.int32) ^ row, piece
        )

    parts = [quarter(row)]
    for step in range(1, size):
        parts.append(send(quarter(row ^ step), across(step)))
    away = pair((3, 1, 2))
    got_far_a = send(away[0], across(1))
    got_far_b = send(away[1], across(2))
    got_near_a = send(away[2], across(1))
    got_near_b = send(away[5], across(2))
    parts = jnp.stack(parts)
    strips = [pick(parts, row ^ level)]
    for step in range(1, size):
        strips.append(
            send(
                pick(parts, row ^ level ^ step),
                lambda r, z, k, step=step: (r, z ^ step, k),
            )
        )
    own_sum_a, own_sum_b = pair((0,))
    last_a = send(away[4] + got_far_a, across(2))
    last_b = send(away[3] + got_far_b, across(1))
    c12 = cross_part(core[None], reflectors, width)
    strips = jnp.stack(strips)
    vectors = jnp.concatenate([pick(strips, level ^ b) for b in range(size)])
    vectors_a, vectors_b = vectors[:, :width], vectors[:, width:]
    vnear_a = send(vectors_a, across(1))
    vnear_b = send(vectors_b, across(2))
    sums_a = own_sum_a + got_near_a + last_a
    sums_b = own_sum_b + got_near_b + last_b
    sums = jnp.concatenate([sums_a, sums_b], axis=1)
    direct = {}
    for q in (0, 1):
        direct[q] = send(sums, lambda r, z, k, q=q: (z, r ^ q, k))
    gram = grams(sums_a, sums_b, vectors).reshape(2, 3 * width // 2, width)
    gram = pick(gram, core) + sibling(pick(gram, 1 - core))
    gram = gram.reshape(size, 3 * width // (2 * size), width)
    part = pick(gram, row)
    for step in range(1, size):
        part = part + send(pick(gram, row ^ step), across(step))
    c12_half = c12
    for step in range(1, size):
        c12_half = c12_half + send(c12, across(step))
    c12_other = sibling(c12_half)
    c12 = jnp.concatenate(
        [
            jnp.where(core == 0, c12_half, c12_other),
            jnp.where(core == 0, c12_other, c12_half),
        ]
    )
    vfar_a = send(jnp.stack([vectors_a, vnear_a]), across(2))
    vfar_b = send(jnp.stack([vectors_b, vnear_b]), across(1))
    near_a = send(sums_a, across(1))
    near_b = send(sums_b, across(2))
    total = part
    for step in range(1, size):
        total = total + send(part, lambda r, z, k, step=step: (r, z ^ step, k))
    pieces = jnp.stack([total] + [send(total, across(step)) for step in range(1, size)])
    spread = jnp.concatenate([pick(pieces, row ^ b) for b in range(size)])
    for q in (2, 3):
        direct[q] = send(sums, lambda r, z, k, q=q: (z, r ^ q, k))
    far_a = send(jnp.stack([sums_a, near_a]), across(2))
    far_b = send(jnp.stack([sums_b, near_b]), across(1))
    paired = sibling(spread)
    gram = jnp.concatenate(
        [jnp.where(core == 0, spread, paired), jnp.where(core == 0, paired, spread)]
    )
    depth = 2 * width
    wide, tall = ((depth, depth), BF16), ((cols, depth), BF16)
    right_high, right_low, vector_high, vector_low, x_high, x_low = column_call(
        vector_column_kernel, (tall,) * 4 + (wide,) * 2, row[None],
        factors, c12, vectors, vnear_a, vnear_b, vfar_a, vfar_b,
    )
    (lead,) = column_call(
        sum_column_kernel, (((cols, depth), F32),), row[None],
        x_high, x_low, sums, near_a, near_b, far_a, far_b,
    )
    high, low = finish_factors(factors, c12, gram, lead, vector_high, vector_low, piece)
    out = vector_update(matrix, reflectors, high, low, piece)
    swapped = [sibling(direct[q]) for q in range(size)]
    for half, sources in (
        (core, [direct[q] for q in range(size)]), (1 - core, swapped)
    ):
        blocks = jnp.stack([half * size + (level ^ q) for q in range(size)])
        out = sum_update(blocks, out, right_high, right_low, sources)
    return out


def spread_block(block, axis, owner):
    block = jnp.where(lax.axis_index(axis) == owner, block, jnp.zeros_like(block))
    return lax.psum(block, axis)


def general_body(matrix, reflectors, factors):
    col_count = matrix.shape[1]
    width = factors.shape[1]
    ratio = lax.axis_size("pcol") // lax.axis_size("prow")
    index = lax.axis_index("pcol")

    def columns(block):
        own = lax.dynamic_slice_in_dim(block, index % ratio * col_count, col_count, 0)
        return spread_block(own, "prow", index // ratio)

    col_vectors = columns(reflectors)
    row_sums = lax.psum(exact(matrix, col_vectors), "pcol")
    col_sums = columns(row_sums)
    first, second = reflectors[:, :width], reflectors[:, width:]
    gram = lax.psum(
        jnp.stack(
            [
                exact(first, row_sums[:, :width], 0, 0),
                exact(first, row_sums[:, width:], 0, 0),
                exact(second, row_sums[:, width:], 0, 0),
                exact(first, second, 0, 0),
            ]
        ),
        "prow",
    )
    x = mixing(factors[0], factors[1], gram[3])
    k = coupling(factors[0], factors[1], gram[3], gram[0], gram[1], gram[2])
    left = exact(col_sums, x) + exact(col_vectors, k)
    right = exact(col_vectors, x, 1, 1)
    return matrix - exact(reflectors, left, 1, 1) - exact(row_sums, right, 1, 1)


def solution(mesh):
    size = mesh.shape["prow"]

    def body(matrix, reflectors, factors):
        piece = matrix.shape[1] // size
        quad = size == 4 and mesh.shape["pcol"] == 2 * size and piece % 128 == 0 and piece % (8 * size) == 0
        return (quad_body if quad else general_body)(matrix, reflectors, factors)

    return jax.shard_map(
        body,
        mesh=mesh,
        in_specs=(P("prow", "pcol"), P("prow", None), P()),
        out_specs=P("prow", "pcol"),
        check_vma=False,
    )
```

profile of v0, /device:TPU:5, one launch (start us, length us, event | category | flops | bytes accessed | tf_op | source)
XLA Modules:
  0.0 315.3 jit_solution(7263204992714942305)
XLA Ops:
  5.2 19.1 %shard_map.57 = (f32[384,256]{1,0:T(8,128)}, f32[384,256]{1,0:T(8,128)}, f32[384,256]{1,0:T(8,128)}, f32[384,256]{1,0:T(8,128)}, f32[384,256]{1,0:T(8,128)}, /*index=5*/f32[384,256]{1,0:T(8,128)}) custom-call(s32[3]{0:T(128)} %broadcast_xor_fusion.slots_ref, f32[3072,512]{1,0:T(8,128)} %vectors_ref.5, f32[3072,1536]{1,0:T(8,128)} %matrix_ref.5), custom_call_target="tpu_custom_call" | custom-call | tf_op jit(solution)/shard_map/pallas_call | solution.py:73
  25.9 3.4 %collective-permute-start.15 = (f32[96,512]{1,0:T(8,128)S(1)}, f32[96,512]{1,0:T(8,128)S(1)}, u32[]{:S(2)}, u32[]{:S(2)}) collective-permute-start(f32[96,512]{1,0:T(8,128)S(1)} %get-tuple-element.52), channel_id=1, source_target_pairs={{0,6},{1,7},{2,4},{3,5},{4,2},{5,3},{6,0},{7,1},{8,14},{9,15},{10,... | collective-permute-start | bytes 589832 | tf_op jit(solution)/shard_map/ppermute | solution.py:326
  29.7 3.9 %shard_map.55 = f32[128,256]{1,0:T(8,128)} custom-call(s32[1]{0:T(128)} %bitcast.8.core_ref, f32[3072,512]{1,0:T(8,128)} %vectors_ref.5, f32[3072,512]{1,0:T(8,128)} %vectors_ref.5), custom_call_target="tpu_custom_call" | custom-call | tf_op jit(solution)/shard_map/pallas_call | solution.py:99
  33.6 9.0 %shard_map.56 = (f32[384,256]{1,0:T(8,128)}, f32[384,256]{1,0:T(8,128)}) custom-call(s32[1]{0:T(128)} %bitcast.9.slots_ref.row_ref, f32[3072,512]{1,0:T(8,128)} %vectors_ref.5, f32[3072,1536]{1,0:T(8,128)} %matrix_ref.5), custom_call_target="tpu_custom_call" | custom-call | tf_op jit(solution)/shard_map/pallas_call | solution.py:73
  48.1 6.1 %collective-permute-done.4 = f32[384,256]{1,0:T(8,128)S(1)} collective-permute-done((f32[384,256]{1,0:T(8,128)}, f32[384,256]{1,0:T(8,128)S(1)}, u32[]{:S(2)}, u32[]{:S(2)}) %collective-permute-start.4) | collective-permute-done | bytes 393248 | tf_op jit(solution)/shard_map/ppermute | solution.py:326
  54.5 9.1 %collective-permute-done.6 = f32[384,256]{1,0:T(8,128)S(1)} collective-permute-done((f32[384,256]{1,0:T(8,128)S(1)}, f32[384,256]{1,0:T(8,128)S(1)}, u32[]{:S(2)}, u32[]{:S(2)}) %collective-permute-start.6) | collective-permute-done | bytes 393248 | tf_op jit(solution)/shard_map/ppermute | solution.py:326
  65.6 3.1 shard_map.58
  69.8 4.7 %collective-permute-start.16 = (f32[384,256]{1,0:T(8,128)S(1)}, f32[384,256]{1,0:T(8,128)S(1)}, u32[]{:S(2)}, u32[]{:S(2)}) collective-permute-start(f32[384,256]{1,0:T(8,128)S(1)} %dynamic-slice_bitcast_fusion), channel_id=1, source_target_pairs={{0,1},{1,0},{2,3},{3,2},{4,5},{5,4},{6,7},{7,6},{8,9},{9,8},{10,11... | collective-permute-start | bytes 1179656 | tf_op jit(solution)/shard_map/ppermute | solution.py:326
  78.8 6.6 %collective-permute-done.27.refs_1_ = f32[384,256]{1,0:T(8,128)S(1)} collective-permute-done((f32[384,256]{1,0:T(8,128)S(1)}, f32[384,256]{1,0:T(8,128)S(1)}, u32[]{:S(2)}, u32[]{:S(2)}) %collective-permute-start.27) | collective-permute-done | bytes 393248 | tf_op jit(solution)/shard_map/ppermute | solution.py:326
  88.7 2.3 collective-permute-done.18
  91.1 3.2 %collective-permute-start.22 = (f32[96,256]{1,0:T(8,128)S(1)}, f32[96,256]{1,0:T(8,128)S(1)}, u32[]{:S(2)}, u32[]{:S(2)}) collective-permute-start(f32[96,256]{1,0:T(8,128)S(1)} %fusion.1), channel_id=1, source_target_pairs={{0,6},{1,7},{2,4},{3,5},{4,2},{5,3},{6,0},{7,1},{8,14},{9,15},{10,... | collective-permute-start | bytes 294920 | tf_op jit(solution)/shard_map/ppermute | solution.py:326
  97.4 4.8 %collective-permute-done.21 = f32[96,256]{1,0:T(8,128)S(1)} collective-permute-done((f32[96,256]{1,0:T(8,128)S(1)}, f32[96,256]{1,0:T(8,128)S(1)}, u32[]{:S(2)}, u32[]{:S(2)}) %collective-permute-start.21) | collective-permute-done | bytes 98336 | tf_op jit(solution)/shard_map/ppermute | solution.py:326
  102.2 3.6 %collective-permute-done.20 = f32[96,256]{1,0:T(8,128)S(1)} collective-permute-done((f32[96,256]{1,0:T(8,128)S(1)}, f32[96,256]{1,0:T(8,128)S(1)}, u32[]{:S(2)}, u32[]{:S(2)}) %collective-permute-start.20) | collective-permute-done | bytes 98336 | tf_op jit(solution)/shard_map/ppermute | solution.py:326
  105.9 2.5 collective-permute-start.35
  108.4 11.6 %collective-permute-done.31.refs_1_ = f32[384,256]{1,0:T(8,128)S(1)} collective-permute-done((f32[384,256]{1,0:T(8,128)S(1)}, f32[384,256]{1,0:T(8,128)S(1)}, u32[]{:S(2)}, u32[]{:S(2)}) %collective-permute-start.31) | collective-permute-done | bytes 393248 | tf_op jit(solution)/shard_map/ppermute | solution.py:326
  120.0 19.5 %collective-permute-start.25 = (f32[96,256]{1,0:T(8,128)S(1)}, f32[96,256]{1,0:T(8,128)S(1)}, u32[]{:S(2)}, u32[]{:S(2)}) collective-permute-start(f32[96,256]{1,0:T(8,128)S(1)} %add_add_fusion.3), channel_id=1, source_target_pairs={{0,24},{1,25},{2,26},{3,27},{4,28},{5,29},{6,30},{7,31},{8,16},{9,... | collective-permute-start | bytes 294920 | tf_op jit(solution)/shard_map/ppermute | solution.py:326
  139.5 3.2 %collective-permute-done.25 = f32[96,256]{1,0:T(8,128)S(1)} collective-permute-done((f32[96,256]{1,0:T(8,128)S(1)}, f32[96,256]{1,0:T(8,128)S(1)}, u32[]{:S(2)}, u32[]{:S(2)}) %collective-permute-start.25) | collective-permute-done | bytes 98336 | tf_op jit(solution)/shard_map/ppermute | solution.py:326
  142.7 7.5 %collective-permute-done.24 = f32[96,256]{1,0:T(8,128)S(1)} collective-permute-done((f32[96,256]{1,0:T(8,128)S(1)}, f32[96,256]{1,0:T(8,128)S(1)}, u32[]{:S(2)}, u32[]{:S(2)}) %collective-permute-start.24) | collective-permute-done | bytes 98336 | tf_op jit(solution)/shard_map/ppermute | solution.py:326
  150.2 9.1 %collective-permute-start.37 = (f32[384,512]{1,0:T(8,128)S(1)}, f32[384,512]{1,0:T(8,128)}, u32[]{:S(2)}, u32[]{:S(2)}) collective-permute-start(f32[384,512]{1,0:T(8,128)S(1)} %pad_maximum_fusion.6.refs_0_), channel_id=1, source_target_pairs={{0,4},{1,5},{2,12},{3,13},{4,20},{5,21},{6,28},{7,29},{8,6},{9,7},... | collective-permute-start | bytes 2359304 | tf_op jit(solution)/shard_map/ppermute | solution.py:326
  159.3 4.2 %collective-permute-start.38 = (f32[384,512]{1,0:T(8,128)S(1)}, f32[384,512]{1,0:T(8,128)}, u32[]{:S(2)}, u32[]{:S(2)}) collective-permute-start(f32[384,512]{1,0:T(8,128)S(1)} %pad_maximum_fusion.6.refs_0_), channel_id=1, source_target_pairs={{0,6},{1,7},{2,14},{3,15},{4,22},{5,23},{6,30},{7,31},{8,4},{9,5},... | collective-permute-start | bytes 2359304 | tf_op jit(solution)/shard_map/ppermute | solution.py:326
  164.4 3.4 %collective-permute-start.33 = (f32[2,384,256]{2,1,0:T(8,128)}, f32[2,384,256]{2,1,0:T(8,128)}, u32[]{:S(2)}, u32[]{:S(2)}) collective-permute-start(f32[2,384,256]{2,1,0:T(8,128)} %pad_maximum_fusion.7), channel_id=1, source_target_pairs={{0,16},{1,17},{2,18},{3,19},{4,20},{5,21},{6,22},{7,23},{8,24},{9,... | collective-permute-start | bytes 2359304 | tf_op jit(solution)/shard_map/ppermute | solution.py:326
  169.6 16.3 %collective-permute-start.26 = (f32[384,256]{1,0:T(8,128)}, f32[384,256]{1,0:T(8,128)}, u32[]{:S(2)}, u32[]{:S(2)}) collective-permute-start(f32[384,256]{1,0:T(8,128)} %pad_maximum_fusion.10), channel_id=1, source_target_pairs={{0,1},{1,0},{2,3},{3,2},{4,5},{5,4},{6,7},{7,6},{8,9},{9,8},{10,11... | collective-permute-start | bytes 1179656 | tf_op jit(solution)/shard_map/ppermute | solution.py:326
  187.8 26.6 %collective-permute-done.37.refs_2_ = f32[384,512]{1,0:T(8,128)} collective-permute-done((f32[384,512]{1,0:T(8,128)S(1)}, f32[384,512]{1,0:T(8,128)}, u32[]{:S(2)}, u32[]{:S(2)}) %collective-permute-start.37) | collective-permute-done | bytes 786464 | tf_op jit(solution)/shard_map/ppermute | solution.py:326
  214.5 3.0 collective-permute-start.39
  217.5 3.4 %collective-permute-done.38.refs_3_ = f32[384,512]{1,0:T(8,128)} collective-permute-done((f32[384,512]{1,0:T(8,128)S(1)}, f32[384,512]{1,0:T(8,128)}, u32[]{:S(2)}, u32[]{:S(2)}) %collective-permute-start.38) | collective-permute-done | bytes 786464 | tf_op jit(solution)/shard_map/ppermute | solution.py:326
  220.8 12.8 %collective-permute-start.40 = (f32[384,512]{1,0:T(8,128)}, f32[384,512]{1,0:T(8,128)}, u32[]{:S(2)}, u32[]{:S(2)}) collective-permute-start(f32[384,512]{1,0:T(8,128)} %collective-permute-done.36.refs_1_), channel_id=1, source_target_pairs={{0,1},{1,0},{2,3},{3,2},{4,5},{5,4},{6,7},{7,6},{8,9},{9,8},{10,11... | collective-permute-start | bytes 2359304 | tf_op jit(solution)/shard_map/ppermute | solution.py:326
  235.6 8.4 %shard_map.59 = (bf16[1536,512]{1,0:T(8,128)(2,1)}, bf16[1536,512]{1,0:T(8,128)(2,1)}, bf16[1536,512]{1,0:T(8,128)(2,1)}, bf16[1536,512]{1,0:T(8,128)(2,1)}, bf1...) custom-call(s32[1]{0:T(128)} %bitcast.9.slots_ref.row_ref, f32[2,256,256]{2,1,0:T(8,128)} %factors_ref.3, ...), custom_call_target="tpu_custom_call" | custom-call | tf_op jit(solution)/shard_map/pallas_call | solution.py:239
  246.0 6.4 %shard_map.60.lead_ref = f32[1536,512]{1,0:T(8,128)} custom-call(s32[1]{0:T(128)} %bitcast.9.slots_ref.row_ref, bf16[512,512]{1,0:T(8,128)(2,1)} %get-tuple-element.29.x_high, bf16[512,512]{1,0:T(8,128)(2,1)} %get-tuple-element.30.x_low, f32[384,512]{1,0:T(8,128)} %copy-done.4, f32[384,256]{1,0:T(8,128)} %copy-done.7, f32[384,256]{1,0:T(8,128)} %copy-done.8, ...), custom_call_target="tpu_custom_call" | custom-call | tf_op jit(solution)/shard_map/pallas_call | solution.py:239
  252.4 10.9 %shard_map.61 = (bf16[1536,512]{1,0:T(8,128)(2,1)}, bf16[1536,512]{1,0:T(8,128)(2,1)}) custom-call(f32[2,256,256]{2,1,0:T(8,128)} %factors_ref.3, f32[256,256]{1,0:T(8,128)} %pad_maximum_fusion.11.c12_ref, f32[768,256]{1,0:T(8,128)} %pad_maximum_fusion.3.gram_ref, f32[1536,512]{1,0:T(8,128)} %shard_map.60.lead_ref, ...), custom_call_target="tpu_custom_call" | custom-call | tf_op jit(solution)/shard_map/pallas_call | solution.py:186
  263.3 23.0 %shard_map.62.matrix_ref = f32[3072,1536]{1,0:T(8,128)} custom-call(f32[3072,1536]{1,0:T(8,128)} %matrix_ref.5, f32[3072,512]{1,0:T(8,128)} %vectors_ref.5, bf16[1536,512]{1,0:T(8,128)(2,1)} %get-tuple-element.33.high_ref, bf16[1536,512]{1,0:T(8,128)(2,1)} %get-tuple-element.34.low_ref), custom_call_target="tpu_custom_call" | custom-call | tf_op jit(solution)/shard_map/pallas_call | solution.py:258
  286.3 14.4 %shard_map.63.matrix_ref = f32[3072,1536]{1,0:T(8,128)} custom-call(s32[4]{0:T(128)} %get-tuple-element.65.block_ref, f32[3072,1536]{1,0:T(8,128)} %shard_map.62.matrix_ref, bf16[1536,512]{1,0:T(8,128)(2,1)} %get-tuple-element.35.high_ref, bf16[1536,512]{1,0:T(8,128)(2,1)} %get-tuple-element.36.low_ref, ...), custom_call_target="tpu_custom_call", output_to_operand_aliasing={{}: (1, {})} | custom-call | tf_op jit(solution)/shard_map/pallas_call | solution.py:292
  300.7 14.6 %shard_map.64 = f32[3072,1536]{1,0:T(8,128)} custom-call(s32[4]{0:T(128)} %get-tuple-element.64.block_ref, f32[3072,1536]{1,0:T(8,128)} %shard_map.63.matrix_ref, bf16[1536,512]{1,0:T(8,128)(2,1)} %get-tuple-element.35.high_ref, bf16[1536,512]{1,0:T(8,128)(2,1)} %get-tuple-element.36.low_ref, ...), custom_call_target="tpu_custom_call", output_to_operand_aliasing={{}: (1, {})} | custom-call | tf_op jit(solution)/shard_map/pallas_call | solution.py:292
  (131 shorter events, 35.3 us)
Async XLA Ops:
  1.3 24.5 %collective-permute-start.12 = (f32[96,512]{1,0:T(8,128)S(1)}, f32[96,512]{1,0:T(8,128)S(1)}, u32[]{:S(2)}, u32[]{:S(2)}) collective-permute-start(f32[96,512]{1,0:T(8,128)S(1)} %get-tuple-element.40), channel_id=1, source_target_pairs={{0,24},{1,25},{2,26},{3,27},{4,28},{5,29},{6,30},{7,31},{8,16},{9,... | collective-permute-start | bytes 589832 | tf_op jit(solution)/shard_map/ppermute | solution.py:326
  2.5 23.3 %collective-permute-start.11 = (f32[96,512]{1,0:T(8,128)S(1)}, f32[96,512]{1,0:T(8,128)S(1)}, u32[]{:S(2)}, u32[]{:S(2)}) collective-permute-start(f32[96,512]{1,0:T(8,128)S(1)} %get-tuple-element.38), channel_id=1, source_target_pairs={{0,16},{1,17},{2,18},{3,19},{4,20},{5,21},{6,22},{7,23},{8,24},{9,... | collective-permute-start | bytes 589832 | tf_op jit(solution)/shard_map/ppermute | solution.py:326
  3.7 22.1 %collective-permute-start.10 = (f32[96,512]{1,0:T(8,128)S(1)}, f32[96,512]{1,0:T(8,128)S(1)}, u32[]{:S(2)}, u32[]{:S(2)}) collective-permute-start(f32[96,512]{1,0:T(8,128)S(1)} %get-tuple-element.39), channel_id=1, source_target_pairs={{0,8},{1,9},{2,10},{3,11},{4,12},{5,13},{6,14},{7,15},{8,0},{9,1},... | collective-permute-start | bytes 589832 | tf_op jit(solution)/shard_map/ppermute | solution.py:326
  24.3 18.3 %collective-permute-start.5 = (f32[384,256]{1,0:T(8,128)}, f32[384,256]{1,0:T(8,128)S(1)}, u32[]{:S(2)}, u32[]{:S(2)}) collective-permute-start(f32[384,256]{1,0:T(8,128)} %get-tuple-element.24), channel_id=1, source_target_pairs={{0,8},{1,9},{2,10},{3,11},{4,12},{5,13},{6,14},{7,15},{8,0},{9,1},... | collective-permute-start | bytes 1179656 | tf_op jit(solution)/shard_map/ppermute | solution.py:326
  25.5 18.3 %collective-permute-start.8 = (f32[384,256]{1,0:T(8,128)}, f32[384,256]{1,0:T(8,128)S(1)}, u32[]{:S(2)}, u32[]{:S(2)}) collective-permute-start(f32[384,256]{1,0:T(8,128)} %get-tuple-element.28), channel_id=1, source_target_pairs={{0,16},{1,17},{2,18},{3,19},{4,20},{5,21},{6,22},{7,23},{8,24},{9,... | collective-permute-start | bytes 1179656 | tf_op jit(solution)/shard_map/ppermute | solution.py:326
  25.9 19.3 %collective-permute-start.15 = (f32[96,512]{1,0:T(8,128)S(1)}, f32[96,512]{1,0:T(8,128)S(1)}, u32[]{:S(2)}, u32[]{:S(2)}) collective-permute-start(f32[96,512]{1,0:T(8,128)S(1)} %get-tuple-element.52), channel_id=1, source_target_pairs={{0,6},{1,7},{2,4},{3,5},{4,2},{5,3},{6,0},{7,1},{8,14},{9,15},{10,... | collective-permute-start | bytes 589832 | tf_op jit(solution)/shard_map/ppermute | solution.py:326
  29.3 16.3 %collective-permute-start.14 = (f32[96,512]{1,0:T(8,128)S(1)}, f32[96,512]{1,0:T(8,128)S(1)}, u32[]{:S(2)}, u32[]{:S(2)}) collective-permute-start(f32[96,512]{1,0:T(8,128)S(1)} %get-tuple-element.53), channel_id=1, source_target_pairs={{0,4},{1,5},{2,6},{3,7},{4,0},{5,1},{6,2},{7,3},{8,12},{9,13},{10,... | collective-permute-start | bytes 589832 | tf_op jit(solution)/shard_map/ppermute | solution.py:326
  29.3 17.5 %collective-permute-start.13 = (f32[96,512]{1,0:T(8,128)S(1)}, f32[96,512]{1,0:T(8,128)S(1)}, u32[]{:S(2)}, u32[]{:S(2)}) collective-permute-start(f32[96,512]{1,0:T(8,128)S(1)} %get-tuple-element.54), channel_id=1, source_target_pairs={{0,2},{1,3},{2,0},{3,1},{4,6},{5,7},{6,4},{7,5},{8,10},{9,11},{10,... | collective-permute-start | bytes 589832 | tf_op jit(solution)/shard_map/ppermute | solution.py:326
  42.6 33.4 %collective-permute-start.2 = (f32[128,256]{1,0:T(8,128)S(1)}, f32[128,256]{1,0:T(8,128)S(1)}, u32[]{:S(2)}, u32[]{:S(2)}) collective-permute-start(f32[128,256]{1,0:T(8,128)S(1)} %copy-done.12), channel_id=1, source_target_pairs={{0,24},{1,25},{2,26},{3,27},{4,28},{5,29},{6,30},{7,31},{8,16},{9,... | collective-permute-start | bytes 393224 | tf_op jit(solution)/shard_map/ppermute | solution.py:326
  45.2 19.6 %collective-permute-start.7 = (f32[384,256]{1,0:T(8,128)S(1)}, f32[384,256]{1,0:T(8,128)S(1)}, u32[]{:S(2)}, u32[]{:S(2)}) collective-permute-start(f32[384,256]{1,0:T(8,128)S(1)} %copy-done.17), channel_id=1, source_target_pairs={{0,16},{1,17},{2,18},{3,19},{4,20},{5,21},{6,22},{7,23},{8,24},{9,... | collective-permute-start | bytes 1179656 | tf_op jit(solution)/shard_map/ppermute | solution.py:326
  45.6 18.0 %collective-permute-start.6 = (f32[384,256]{1,0:T(8,128)S(1)}, f32[384,256]{1,0:T(8,128)S(1)}, u32[]{:S(2)}, u32[]{:S(2)}) collective-permute-start(f32[384,256]{1,0:T(8,128)S(1)} %add.176), channel_id=1, source_target_pairs={{0,16},{1,17},{2,18},{3,19},{4,20},{5,21},{6,22},{7,23},{8,24},{9,... | collective-permute-start | bytes 1179656 | tf_op jit(solution)/shard_map/ppermute | solution.py:326
  46.8 17.9 %collective-permute-start.9 = (f32[384,256]{1,0:T(8,128)S(1)}, f32[384,256]{1,0:T(8,128)S(1)}, u32[]{:S(2)}, u32[]{:S(2)}) collective-permute-start(f32[384,256]{1,0:T(8,128)S(1)} %add.179), channel_id=1, source_target_pairs={{0,8},{1,9},{2,10},{3,11},{4,12},{5,13},{6,14},{7,15},{8,0},{9,1},... | collective-permute-start | bytes 1179656 | tf_op jit(solution)/shard_map/ppermute | solution.py:326
  54.2 21.7 %collective-permute-start.1 = (f32[128,256]{1,0:T(8,128)S(1)}, f32[128,256]{1,0:T(8,128)S(1)}, u32[]{:S(2)}, u32[]{:S(2)}) collective-permute-start(f32[128,256]{1,0:T(8,128)S(1)} %copy-done.12), channel_id=1, source_target_pairs={{0,16},{1,17},{2,18},{3,19},{4,20},{5,21},{6,22},{7,23},{8,24},{9,... | collective-permute-start | bytes 393224 | tf_op jit(solution)/shard_map/ppermute | solution.py:326
  76.0 18.7 %collective-permute-start.3 = (f32[128,256]{1,0:T(8,128)S(1)}, f32[128,256]{1,0:T(8,128)S(1)}, u32[]{:S(2)}, u32[]{:S(2)}) collective-permute-start(f32[128,256]{1,0:T(8,128)S(1)} %add_add_fusion.2), channel_id=1, source_target_pairs={{0,1},{1,0},{2,3},{3,2},{4,5},{5,4},{6,7},{7,6},{8,9},{9,8},{10,11... | collective-permute-start | bytes 393224 | tf_op jit(solution)/shard_map/ppermute | solution.py:326
  76.4 18.0 %collective-permute-start.28 = (f32[384,256]{1,0:T(8,128)S(1)}, f32[384,256]{1,0:T(8,128)S(1)}, u32[]{:S(2)}, u32[]{:S(2)}) collective-permute-start(f32[384,256]{1,0:T(8,128)S(1)} %get-tuple-element.43), channel_id=1, source_target_pairs={{0,16},{1,17},{2,18},{3,19},{4,20},{5,21},{6,22},{7,23},{8,24},{9,... | collective-permute-start | bytes 1179656 | tf_op jit(solution)/shard_map/ppermute | solution.py:326
  78.0 13.1 %collective-permute-start.18 = (f32[96,256]{1,0:T(8,128)S(1)}, f32[96,256]{1,0:T(8,128)S(1)}, u32[]{:S(2)}, u32[]{:S(2)}) collective-permute-start(f32[96,256]{1,0:T(8,128)S(1)} %get-tuple-element.61), channel_id=1, source_target_pairs={{0,16},{1,17},{2,18},{3,19},{4,20},{5,21},{6,22},{7,23},{8,24},{9,... | collective-permute-start | bytes 294920 | tf_op jit(solution)/shard_map/ppermute | solution.py:326
  88.1 71.2 %collective-permute-start.29 = (f32[2,384,256]{2,1,0:T(8,128)S(1)}, f32[2,384,256]{2,1,0:T(8,128)S(1)}, u32[]{:S(2)}, u32[]{:S(2)}) collective-permute-start(f32[2,384,256]{2,1,0:T(8,128)S(1)} %pad_maximum_fusion.4), channel_id=1, source_target_pairs={{0,16},{1,17},{2,18},{3,19},{4,20},{5,21},{6,22},{7,23},{8,24},{9,... | collective-permute-start | bytes 2359304 | tf_op jit(solution)/shard_map/ppermute | solution.py:326
  94.4 70.0 %collective-permute-start.30 = (f32[2,384,256]{2,1,0:T(8,128)S(1)}, f32[2,384,256]{2,1,0:T(8,128)S(1)}, u32[]{:S(2)}, u32[]{:S(2)}) collective-permute-start(f32[2,384,256]{2,1,0:T(8,128)S(1)} %pad_maximum_fusion.5), channel_id=1, source_target_pairs={{0,8},{1,9},{2,10},{3,11},{4,12},{5,13},{6,14},{7,15},{8,0},{9,1},... | collective-permute-start | bytes 2359304 | tf_op jit(solution)/shard_map/ppermute | solution.py:326
  94.7 25.3 %collective-permute-start.31 = (f32[384,256]{1,0:T(8,128)S(1)}, f32[384,256]{1,0:T(8,128)S(1)}, u32[]{:S(2)}, u32[]{:S(2)}) collective-permute-start(f32[384,256]{1,0:T(8,128)S(1)} %copy-done.2), channel_id=1, source_target_pairs={{0,8},{1,9},{2,10},{3,11},{4,12},{5,13},{6,14},{7,15},{8,0},{9,1},... | collective-permute-start | bytes 1179656 | tf_op jit(solution)/shard_map/ppermute | solution.py:326
  96.5 43.0 %collective-permute-start.32 = (f32[384,256]{1,0:T(8,128)S(1)}, f32[384,256]{1,0:T(8,128)S(1)}, u32[]{:S(2)}, u32[]{:S(2)}) collective-permute-start(f32[384,256]{1,0:T(8,128)S(1)} %copy-done.1), channel_id=1, source_target_pairs={{0,16},{1,17},{2,18},{3,19},{4,20},{5,21},{6,22},{7,23},{8,24},{9,... | collective-permute-start | bytes 1179656 | tf_op jit(solution)/shard_map/ppermute | solution.py:326
  105.9 62.8 %collective-permute-start.35 = (f32[384,512]{1,0:T(8,128)S(1)}, f32[384,512]{1,0:T(8,128)S(1)}, u32[]{:S(2)}, u32[]{:S(2)}) collective-permute-start(f32[384,512]{1,0:T(8,128)S(1)} %pad_maximum_fusion.6.refs_0_), channel_id=1, source_target_pairs={{0,0},{1,1},{2,8},{3,9},{4,16},{5,17},{6,24},{7,25},{8,2},{9,3},{1... | collective-permute-start | bytes 2359304 | tf_op jit(solution)/shard_map/ppermute | solution.py:326
  120.0 22.6 %collective-permute-start.25 = (f32[96,256]{1,0:T(8,128)S(1)}, f32[96,256]{1,0:T(8,128)S(1)}, u32[]{:S(2)}, u32[]{:S(2)}) collective-permute-start(f32[96,256]{1,0:T(8,128)S(1)} %add_add_fusion.3), channel_id=1, source_target_pairs={{0,24},{1,25},{2,26},{3,27},{4,28},{5,29},{6,30},{7,31},{8,16},{9,... | collective-permute-start | bytes 294920 | tf_op jit(solution)/shard_map/ppermute | solution.py:326
  150.2 37.0 %collective-permute-start.36 = (f32[384,512]{1,0:T(8,128)S(1)}, f32[384,512]{1,0:T(8,128)}, u32[]{:S(2)}, u32[]{:S(2)}) collective-permute-start(f32[384,512]{1,0:T(8,128)S(1)} %pad_maximum_fusion.6.refs_0_), channel_id=1, source_target_pairs={{0,2},{1,3},{2,10},{3,11},{4,18},{5,19},{6,26},{7,27},{8,0},{9,1},... | collective-permute-start | bytes 2359304 | tf_op jit(solution)/shard_map/ppermute | solution.py:326
  150.2 64.3 %collective-permute-start.37 = (f32[384,512]{1,0:T(8,128)S(1)}, f32[384,512]{1,0:T(8,128)}, u32[]{:S(2)}, u32[]{:S(2)}) collective-permute-start(f32[384,512]{1,0:T(8,128)S(1)} %pad_maximum_fusion.6.refs_0_), channel_id=1, source_target_pairs={{0,4},{1,5},{2,12},{3,13},{4,20},{5,21},{6,28},{7,29},{8,6},{9,7},... | collective-permute-start | bytes 2359304 | tf_op jit(solution)/shard_map/ppermute | solution.py:326
  159.3 61.6 %collective-permute-start.38 = (f32[384,512]{1,0:T(8,128)S(1)}, f32[384,512]{1,0:T(8,128)}, u32[]{:S(2)}, u32[]{:S(2)}) collective-permute-start(f32[384,512]{1,0:T(8,128)S(1)} %pad_maximum_fusion.6.refs_0_), channel_id=1, source_target_pairs={{0,6},{1,7},{2,14},{3,15},{4,22},{5,23},{6,30},{7,31},{8,4},{9,5},... | collective-permute-start | bytes 2359304 | tf_op jit(solution)/shard_map/ppermute | solution.py:326
  164.4 69.3 %collective-permute-start.33 = (f32[2,384,256]{2,1,0:T(8,128)}, f32[2,384,256]{2,1,0:T(8,128)}, u32[]{:S(2)}, u32[]{:S(2)}) collective-permute-start(f32[2,384,256]{2,1,0:T(8,128)} %pad_maximum_fusion.7), channel_id=1, source_target_pairs={{0,16},{1,17},{2,18},{3,19},{4,20},{5,21},{6,22},{7,23},{8,24},{9,... | collective-permute-start | bytes 2359304 | tf_op jit(solution)/shard_map/ppermute | solution.py:326
  169.6 64.0 %collective-permute-start.26 = (f32[384,256]{1,0:T(8,128)}, f32[384,256]{1,0:T(8,128)}, u32[]{:S(2)}, u32[]{:S(2)}) collective-permute-start(f32[384,256]{1,0:T(8,128)} %pad_maximum_fusion.10), channel_id=1, source_target_pairs={{0,1},{1,0},{2,3},{3,2},{4,5},{5,4},{6,7},{7,6},{8,9},{9,8},{10,11... | collective-permute-start | bytes 1179656 | tf_op jit(solution)/shard_map/ppermute | solution.py:326
  187.2 58.8 %collective-permute-start.34 = (f32[2,384,256]{2,1,0:T(8,128)S(1)}, f32[2,384,256]{2,1,0:T(8,128)}, u32[]{:S(2)}, u32[]{:S(2)}) collective-permute-start(f32[2,384,256]{2,1,0:T(8,128)S(1)} %pad_maximum_fusion.8), channel_id=1, source_target_pairs={{0,8},{1,9},{2,10},{3,11},{4,12},{5,13},{6,14},{7,15},{8,0},{9,1},... | collective-permute-start | bytes 2359304 | tf_op jit(solution)/shard_map/ppermute | solution.py:326
  214.5 86.2 %collective-permute-start.39 = (f32[384,512]{1,0:T(8,128)}, f32[384,512]{1,0:T(8,128)}, u32[]{:S(2)}, u32[]{:S(2)}) collective-permute-start(f32[384,512]{1,0:T(8,128)} %copy-done.11), channel_id=1, source_target_pairs={{0,1},{1,0},{2,3},{3,2},{4,5},{5,4},{6,7},{7,6},{8,9},{9,8},{10,11... | collective-permute-start | bytes 2359304 | tf_op jit(solution)/shard_map/ppermute | solution.py:326
  220.8 79.8 %collective-permute-start.40 = (f32[384,512]{1,0:T(8,128)}, f32[384,512]{1,0:T(8,128)}, u32[]{:S(2)}, u32[]{:S(2)}) collective-permute-start(f32[384,512]{1,0:T(8,128)} %collective-permute-done.36.refs_1_), channel_id=1, source_target_pairs={{0,1},{1,0},{2,3},{3,2},{4,5},{5,4},{6,7},{7,6},{8,9},{9,8},{10,11... | collective-permute-start | bytes 2359304 | tf_op jit(solution)/shard_map/ppermute | solution.py:326
  233.7 67.0 %collective-permute-start.41 = (f32[384,512]{1,0:T(8,128)}, f32[384,512]{1,0:T(8,128)}, u32[]{:S(2)}, u32[]{:S(2)}) collective-permute-start(f32[384,512]{1,0:T(8,128)} %collective-permute-done.37.refs_2_), channel_id=1, source_target_pairs={{0,1},{1,0},{2,3},{3,2},{4,5},{5,4},{6,7},{7,6},{8,9},{9,8},{10,11... | collective-permute-start | bytes 2359304 | tf_op jit(solution)/shard_map/ppermute | solution.py:326
  233.7 67.0 %collective-permute-start.42 = (f32[384,512]{1,0:T(8,128)}, f32[384,512]{1,0:T(8,128)}, u32[]{:S(2)}, u32[]{:S(2)}) collective-permute-start(f32[384,512]{1,0:T(8,128)} %collective-permute-done.38.refs_3_), channel_id=1, source_target_pairs={{0,1},{1,0},{2,3},{3,2},{4,5},{5,4},{6,7},{7,6},{8,9},{9,8},{10,11... | collective-permute-start | bytes 2359304 | tf_op jit(solution)/shard_map/ppermute | solution.py:326
  (29 other events, 745.4 us)
where the time goes:
time: 316 us; the launch traced here: 315 us
  Pallas kernels  113 us (36%)
  starting transfers between devices  101 us (32%)
  waiting for transfers between devices  88.1 us (28%)
  other arithmetic  9.55 us (3%)
  local copies, waits for them, and re-layouts  3.69 us (1%)
    ppermute x43, starting transfers between devices, send(): return lax.ppermute(value, AXES, pairs)  101 us
    ppermute x43, waiting for transfers between devices, send(): return lax.ppermute(value, AXES, pairs)  88.1 us
    pallas_call x2, Pallas kernels, sum_update(): pl.pallas_call(functools.partial(sum_update_kernel, sources=count), grid_...  29 us
    pallas_call x2, Pallas kernels, pair_sums(): pl.pallas_call(pair_kernel, grid_spec=pltpu.PrefetchScalarGridSpec(num_sc...  28.1 us
    pallas_call x1, Pallas kernels, vector_update(): pl.pallas_call(vector_update_kernel, grid=(rows // piece,), in_specs=[pl....  23 us
    pallas_call x2, Pallas kernels, column_call(): pl.pallas_call(kernel, in_specs=[pl.BlockSpec(memory_space=pltpu.SMEM)] +...  14.8 us
    pallas_call x1, Pallas kernels, finish_factors(): pl.pallas_call(finish_kernel, grid=(cols // piece,), in_specs=[pl.BlockSp...  10.9 us
  transfers between devices with their start and end apart: 43, of which 15 were waited for; matrix products, arithmetic and copies ran while one was open for 3% of the time, Pallas kernels for 31%

commit v1 on v0

--- a/solution.py
+++ b/solution.py
@@ -143,24 +143,62 @@
     return jnp.concatenate([top, bottom])
 
 
-def coupling(first, second, c12, g11, g12, g22):
-    t1_c = exact(first, c12)
-    m1 = exact(first, exact(g11, first), 0, 0)
-    half_m1_c = 0.5 * exact(m1, c12)
-    lead = half_m1_c - (exact(first, g12, 0, 0) - 0.5 * exact(m1, c12, 0, 0))
-    inner = g22 - exact(g12, t1_c, 0, 0) + exact(c12, lead, 0, 0)
-    m2 = exact(second, exact(inner, second), 0, 0)
-    cross = exact(lead, second)
+def coupling(first, second, c12, g11, g12, g22, dot):
+    t1_c = dot(first, c12)
+    m1 = dot(first, dot(g11, first), 0, 0)
+    half_m1_c = 0.5 * dot(m1, c12)
+    lead = half_m1_c - (dot(first, g12, 0, 0) - 0.5 * dot(m1, c12, 0, 0))
+    inner = g22 - dot(g12, t1_c, 0, 0) + dot(c12, lead, 0, 0)
+    m2 = dot(second, dot(inner, second), 0, 0)
+    cross = dot(lead, second)
     top = jnp.concatenate([-0.5 * (m1 + m1.T), cross], axis=1)
     bottom = jnp.concatenate([cross.T, -0.5 * (m2 + m2.T)], axis=1)
     return jnp.concatenate([top, bottom])
 
 
-def finish_kernel(factors_ref, c12_ref, gram_ref, lead_ref, high_ref, low_ref, *refs):
-    out_high, out_low, k_high, k_low = refs
+def split_dot(left, right, left_dim=1, right_dim=0):
+    return contract_split(halves(left), halves(right), left_dim, right_dim)
+
+
+def choose_kernel(index_ref, *refs, count):
+    sources, outs, held_ref = refs[:-1 - count], refs[-1 - count : -1], refs[-1]
+    for number, source in enumerate(sources):
+
+        @pl.when(index_ref[pl.program_id(0)] == number)
+        def _(source=source):
+            held_ref[...] = source[...]
+
+    for number, out in enumerate(outs):
+
+        @pl.when(pl.program_id(0) == number)
+        def _(out=out):
+            out[...] = held_ref[...]
+
+
+def choose(index, sources):
+    count = index.shape[0]
+    shape = sources[0].shape
+    whole = pl.BlockSpec(shape, lambda j, i: (0, 0), pipeline_mode=pl.Buffered(1))
+    return pl.pallas_call(
+        functools.partial(choose_kernel, count=count),
+        grid_spec=pltpu.PrefetchScalarGridSpec(
+            num_scalar_prefetch=1,
+            grid=(count,),
+            in_specs=[whole] * len(sources),
+            out_specs=(pl.BlockSpec(shape, lambda j, i: (0, 0)),) * count,
+            scratch_shapes=[pltpu.VMEM(shape, F32)],
+        ),
+        out_shape=(jax.ShapeDtypeStruct(shape, F32),) * count,
+        compiler_params=params(),
+    )(index, *sources)
+
+
+def finish_kernel(row_ref, factors_ref, c12_ref, gram_ref, x_high, x_low, *refs):
+    vector_high, vector_low, out_high, out_low, k_high, k_low, sums_ref = refs[5:]
     width = factors_ref.shape[1]
-
-    @pl.when(pl.program_id(0) == 0)
+    slot = pl.program_id(0)
+
+    @pl.when(slot == 0)
     def _():
         k = coupling(
             factors_ref[0],
@@ -169,36 +207,56 @@
             gram_ref[:width, :],
             gram_ref[width : 2 * width, :],
             gram_ref[2 * width :, :],
+            split_dot,
         )
         k_high[...], k_low[...] = halves(k)
 
-    value = lead_ref[...] + contract_split(
-        (high_ref[...], low_ref[...]), (k_high[...], k_low[...]), 1, 0
+    for index, parts in enumerate(slot_refs(refs[:5])):
+
+        @pl.when(slot == index)
+        def _(parts=parts):
+            at = 0
+            for ref, lead in parts:
+                value = ref[...] if lead is None else ref[lead]
+                sums_ref[:, at : at + value.shape[1]] = value
+                at += value.shape[1]
+
+    value = contract_split(
+        halves(sums_ref[...]), (x_high[...], x_low[...]), 1, 0
+    ) + contract_split(
+        (vector_high[...], vector_low[...]), (k_high[...], k_low[...]), 1, 0
     )
     out_high[...], out_low[...] = halves(value)
 
 
-def finish_factors(factors, c12, gram, lead, high, low, piece):
-    cols, depth = lead.shape
-    width = factors.shape[1]
-    tile = pl.BlockSpec((piece, depth), lambda j: (j, 0))
+def finish_factors(row, factors, c12, gram, x_high, x_low, parts, high, low, piece):
+    cols, depth = high.shape
+    tile = pl.BlockSpec((piece, depth), lambda j, r: (r[0] ^ j, 0))
     shape = jax.ShapeDtypeStruct((cols, depth), BF16)
+    whole = pl.BlockSpec(memory_space=pltpu.VMEM)
     return pl.pallas_call(
         finish_kernel,
-        grid=(cols // piece,),
-        in_specs=[
-            pl.BlockSpec((2, width, width), lambda j: (0, 0, 0)),
-            pl.BlockSpec((width, width), lambda j: (0, 0)),
-            pl.BlockSpec((3 * width, width), lambda j: (0, 0)),
-            tile,
-            tile,
-            tile,
-        ],
-        out_specs=(tile, tile),
+        grid_spec=pltpu.PrefetchScalarGridSpec(
+            num_scalar_prefetch=1,
+            grid=(cols // piece,),
+            in_specs=[whole] * (5 + len(parts)) + [tile, tile],
+            out_specs=(tile, tile),
+            scratch_shapes=[pltpu.VMEM((depth, depth), BF16)] * 2
+            + [pltpu.VMEM((piece, depth), F32)],
+        ),
         out_shape=(shape, shape),
-        scratch_shapes=[pltpu.VMEM((depth, depth), BF16)] * 2,
-        compiler_params=params(),
-    )(factors, c12, gram, lead, high, low)
+        compiler_params=params(),
+    )(row, factors, c12, gram, x_high, x_low, *parts, high, low)
+
+
+def slot_refs(refs):
+    own, near_a, near_b, far_a, far_b = refs
+    return (
+        ((own, None),),
+        ((near_a, None), (far_b, 0)),
+        ((far_a, 0), (near_b, None)),
+        ((far_a, 1), (far_b, 1)),
+    )
 
 
 def slot_pieces(refs):
@@ -225,13 +283,6 @@
         at = rows_of(row_ref, slot, piece)
         right_high[at, :], right_low[at, :] = halves(contract_split(vectors, x, 1, 1))
         vector_high[at, :], vector_low[at, :] = vectors
-
-
-def sum_column_kernel(row_ref, x_high, x_low, *refs):
-    piece = refs[0].shape[0]
-    x = (x_high[...], x_low[...])
-    for slot, value in enumerate(slot_pieces(refs[:5])):
-        refs[5][rows_of(row_ref, slot, piece), :] = contract_split(halves(value), x, 1, 0)
 
 
 def column_call(kernel, shapes, row, *args):
@@ -374,9 +425,24 @@
     sums_a = own_sum_a + got_near_a + last_a
     sums_b = own_sum_b + got_near_b + last_b
     sums = jnp.concatenate([sums_a, sums_b], axis=1)
-    direct = {}
-    for q in (0, 1):
-        direct[q] = send(sums, lambda r, z, k, q=q: (z, r ^ q, k))
+    ups, downs = [sums], [sums]
+    for step in range(1, size):
+        ups.append(
+            send(
+                ups[-1],
+                lambda r, z, k, step=step: (r, z + 1, k)
+                if step - 1 <= z < size - 1
+                else None,
+            )
+        )
+        downs.append(
+            send(
+                downs[-1],
+                lambda r, z, k, step=step: (r, z - 1, k)
+                if 0 < z <= size - step
+                else None,
+            )
+        )
     gram = grams(sums_a, sums_b, vectors).reshape(2, 3 * width // 2, width)
     gram = pick(gram, core) + sibling(pick(gram, 1 - core))
     gram = gram.reshape(size, 3 * width // (2 * size), width)
@@ -402,8 +468,6 @@
         total = total + send(part, lambda r, z, k, step=step: (r, z ^ step, k))
     pieces = jnp.stack([total] + [send(total, across(step)) for step in range(1, size)])
     spread = jnp.concatenate([pick(pieces, row ^ b) for b in range(size)])
-    for q in (2, 3):
-        direct[q] = send(sums, lambda r, z, k, q=q: (z, r ^ q, k))
     far_a = send(jnp.stack([sums_a, near_a]), across(2))
     far_b = send(jnp.stack([sums_b, near_b]), across(1))
     paired = sibling(spread)
@@ -416,17 +480,19 @@
         vector_column_kernel, (tall,) * 4 + (wide,) * 2, row[None],
         factors, c12, vectors, vnear_a, vnear_b, vfar_a, vfar_b,
     )
-    (lead,) = column_call(
-        sum_column_kernel, (((cols, depth), F32),), row[None],
-        x_high, x_low, sums, near_a, near_b, far_a, far_b,
-    )
-    high, low = finish_factors(factors, c12, gram, lead, vector_high, vector_low, piece)
+    high, low = finish_factors(
+        row[None], factors, c12, gram, x_high, x_low,
+        (sums, near_a, near_b, far_a, far_b), vector_high, vector_low, piece,
+    )
     out = vector_update(matrix, reflectors, high, low, piece)
+    wanted = (jnp.arange(size, dtype=jnp.int32) ^ row) - level + size - 1
+    chosen = choose(wanted, ups[:0:-1] + [sums] + downs[1:])
+    direct = [chosen[0]] + [send(chosen[m], across(m)) for m in range(1, size)]
     swapped = [sibling(direct[q]) for q in range(size)]
     for half, sources in (
         (core, [direct[q] for q in range(size)]), (1 - core, swapped)
     ):
-        blocks = jnp.stack([half * size + (level ^ q) for q in range(size)])
+        blocks = jnp.stack([half * size + (row ^ m) for m in range(size)])
         out = sum_update(blocks, out, right_high, right_low, sources)
     return out
 
@@ -462,7 +528,9 @@
         "prow",
     )
     x = mixing(factors[0], factors[1], gram[3])
-    k = coupling(factors[0], factors[1], gram[3], gram[0], gram[1], gram[2])
+    k = coupling(
+        factors[0], factors[1], gram[3], gram[0], gram[1], gram[2], exact
+    )
     left = exact(col_sums, x) + exact(col_vectors, k)
     right = exact(col_vectors, x, 1, 1)
     return matrix - exact(reflectors, left, 1, 1) - exact(row_sums, right, 1, 1)

time: 316 us -> 285 us (0.902)
  the two profiles are of different devices: /device:TPU:5 before, /device:TPU:0 now
where the time goes in v1:
time: 285 us
  Pallas kernels  113 us (40%)
  waiting for transfers between devices  85.5 us (30%)
  starting transfers between devices  63.6 us (22%)
  other arithmetic  14.6 us (5%)
  local copies, waits for them, and re-layouts  7.05 us (2%)
    ppermute x48, waiting for transfers between devices, send(): return lax.ppermute(value, AXES, pairs)  85.5 us
    ppermute x48, starting transfers between devices, send(): return lax.ppermute(value, AXES, pairs)  63.6 us
    pallas_call x2, Pallas kernels, sum_update(): pl.pallas_call(functools.partial(sum_update_kernel, sources=count), grid_...  29 us
    pallas_call x2, Pallas kernels, pair_sums(): pl.pallas_call(pair_kernel, grid_spec=pltpu.PrefetchScalarGridSpec(num_sc...  28.1 us
    pallas_call x1, Pallas kernels, vector_update(): pl.pallas_call(vector_update_kernel, grid=(rows // piece,), in_specs=[pl....  23 us
    pallas_call x1, Pallas kernels, finish_factors(): pl.pallas_call(finish_kernel, grid_spec=pltpu.PrefetchScalarGridSpec(num_...  12.2 us
    pallas_call x1, Pallas kernels, column_call(): pl.pallas_call(kernel, in_specs=[pl.BlockSpec(memory_space=pltpu.SMEM)] +...  8.47 us
  transfers between devices with their start and end apart: 48, of which 14 were waited for; matrix products, arithmetic and copies ran while one was open for 7% of the time, Pallas kernels for 28%

profile of v1, /device:TPU:0, one launch (start us, length us, event | category | flops | bytes accessed | tf_op | source)
XLA Modules:
  0.0 284.5 jit_solution(18383141533711608206)
XLA Ops:
  1.2 19.1 %shard_map.57 = (f32[384,256]{1,0:T(8,128)}, f32[384,256]{1,0:T(8,128)}, f32[384,256]{1,0:T(8,128)}, f32[384,256]{1,0:T(8,128)}, f32[384,256]{1,0:T(8,128)}, /*index=5*/f32[384,256]{1,0:T(8,128)}) custom-call(s32[3]{0:T(128)} %broadcast_xor_fusion.slots_ref, f32[3072,512]{1,0:T(8,128)} %vectors_ref.5, f32[3072,1536]{1,0:T(8,128)} %matrix_ref.5), custom_call_target="tpu_custom_call" | custom-call | tf_op jit(solution)/shard_map/pallas_call | solution.py:73
  20.3 3.0 %collective-permute-start.5 = (f32[384,256]{1,0:T(8,128)}, f32[384,256]{1,0:T(8,128)S(1)}, u32[]{:S(2)}, u32[]{:S(2)}) collective-permute-start(f32[384,256]{1,0:T(8,128)} %get-tuple-element.28), channel_id=1, source_target_pairs={{0,8},{1,9},{2,10},{3,11},{4,12},{5,13},{6,14},{7,15},{8,0},{9,1},... | collective-permute-start | bytes 1179656 | tf_op jit(solution)/shard_map/ppermute | solution.py:377
  26.1 2.0 collective-permute-start.11
  29.6 3.9 %collective-permute-done.5 = f32[384,256]{1,0:T(8,128)S(1)} collective-permute-done((f32[384,256]{1,0:T(8,128)}, f32[384,256]{1,0:T(8,128)S(1)}, u32[]{:S(2)}, u32[]{:S(2)}) %collective-permute-start.5) | collective-permute-done | bytes 393248 | tf_op jit(solution)/shard_map/ppermute | solution.py:377
  33.5 2.0 collective-permute-start.4
  36.6 3.2 %collective-permute-done.8 = f32[384,256]{1,0:T(8,128)S(1)} collective-permute-done((f32[384,256]{1,0:T(8,128)}, f32[384,256]{1,0:T(8,128)S(1)}, u32[]{:S(2)}, u32[]{:S(2)}) %collective-permute-start.8) | collective-permute-done | bytes 393248 | tf_op jit(solution)/shard_map/ppermute | solution.py:377
  41.2 8.9 %shard_map.56 = (f32[384,256]{1,0:T(8,128)}, f32[384,256]{1,0:T(8,128)}) custom-call(s32[1]{0:T(128)} %bitcast.8.slots_ref.row_ref, f32[3072,512]{1,0:T(8,128)} %vectors_ref.5, f32[3072,1536]{1,0:T(8,128)} %matrix_ref.5), custom_call_target="tpu_custom_call" | custom-call | tf_op jit(solution)/shard_map/pallas_call | solution.py:73
  51.0 3.7 %collective-permute-start.15 = (f32[96,512]{1,0:T(8,128)S(1)}, f32[96,512]{1,0:T(8,128)S(1)}, u32[]{:S(2)}, u32[]{:S(2)}) collective-permute-start(f32[96,512]{1,0:T(8,128)S(1)} %get-tuple-element.60), channel_id=1, source_target_pairs={{0,6},{1,7},{2,4},{3,5},{4,2},{5,3},{6,0},{7,1},{8,14},{9,15},{10,... | collective-permute-start | bytes 589832 | tf_op jit(solution)/shard_map/ppermute | solution.py:377
  56.6 2.8 collective-permute-done.7
  60.6 4.4 %collective-permute-start.35 = (f32[384,512]{1,0:T(8,128)S(1)}, f32[384,512]{1,0:T(8,128)}, u32[]{:S(2)}, u32[]{:S(2)}) collective-permute-start(f32[384,512]{1,0:T(8,128)S(1)} %pad_maximum_fusion.6.refs_0_.refs_3_), channel_id=1, source_target_pairs={{0,2},{1,3},{2,4},{3,5},{4,6},{5,7},{8,10},{9,11},{10,12},{11,13},... | collective-permute-start | bytes 2359304 | tf_op jit(solution)/shard_map/ppermute | solution.py:377
  66.3 3.9 %shard_map.55 = f32[128,256]{1,0:T(8,128)} custom-call(s32[1]{0:T(128)} %bitcast.9.core_ref, f32[3072,512]{1,0:T(8,128)} %vectors_ref.5, f32[3072,512]{1,0:T(8,128)} %vectors_ref.5), custom_call_target="tpu_custom_call" | custom-call | tf_op jit(solution)/shard_map/pallas_call | solution.py:99
  74.9 3.1 %shard_map.58 = f32[768,256]{1,0:T(8,128)} custom-call(f32[384,256]{1,0:T(8,128)} %copy-done.3, f32[384,256]{1,0:T(8,128)} %copy-done.1, f32[384,512]{1,0:T(8,128)} %pad_maximum_fusion.2.vectors_ref.refs_0_), custom_call_target="tpu_custom_call" | custom-call | tf_op jit(solution)/shard_map/pallas_call | solution.py:128
  81.3 1.8 collective-permute-done.38.refs_4_
  84.6 2.0 slice_bitcast_fusion
  89.4 2.8 collective-permute-start.19
  92.2 4.7 %collective-permute-done.27.refs_1_ = f32[384,256]{1,0:T(8,128)S(1)} collective-permute-done((f32[384,256]{1,0:T(8,128)S(1)}, f32[384,256]{1,0:T(8,128)S(1)}, u32[]{:S(2)}, u32[]{:S(2)}) %collective-permute-start.27) | collective-permute-done | bytes 393248 | tf_op jit(solution)/shard_map/ppermute | solution.py:377
  101.3 7.2 %collective-permute-done.17 = f32[96,256]{1,0:T(8,128)S(1)} collective-permute-done((f32[96,256]{1,0:T(8,128)}, f32[96,256]{1,0:T(8,128)S(1)}, u32[]{:S(2)}, u32[]{:S(2)}) %collective-permute-start.17) | collective-permute-done | bytes 98336 | tf_op jit(solution)/shard_map/ppermute | solution.py:377
  112.9 5.5 %collective-permute-start.22 = (f32[96,256]{1,0:T(8,128)S(1)}, f32[96,256]{1,0:T(8,128)S(1)}, u32[]{:S(2)}, u32[]{:S(2)}) collective-permute-start(f32[96,256]{1,0:T(8,128)S(1)} %fusion.1), channel_id=1, source_target_pairs={{0,6},{1,7},{2,4},{3,5},{4,2},{5,3},{6,0},{7,1},{8,14},{9,15},{10,... | collective-permute-start | bytes 294920 | tf_op jit(solution)/shard_map/ppermute | solution.py:377
  120.0 1.9 collective-permute-done.22
  124.2 1.8 collective-permute-start.20
  126.1 11.2 %collective-permute-done.20 = f32[96,256]{1,0:T(8,128)S(1)} collective-permute-done((f32[96,256]{1,0:T(8,128)S(1)}, f32[96,256]{1,0:T(8,128)S(1)}, u32[]{:S(2)}, u32[]{:S(2)}) %collective-permute-start.20) | collective-permute-done | bytes 98336 | tf_op jit(solution)/shard_map/ppermute | solution.py:377
  144.2 5.6 %shard_map.62 = (f32[384,512]{1,0:T(8,128)}, f32[384,512]{1,0:T(8,128)}, f32[384,512]{1,0:T(8,128)}, f32[384,512]{1,0:T(8,128)}) custom-call(s32[4]{0:T(128)} %subtract_add_fusion.index_ref, f32[384,512]{1,0:T(8,128)} %copy-done.13, f32[384,512]{1,0:T(8,128)} %collective-permute-done.36.refs_1_, f32[384,512]{1,0:T(8,128)} %collective-permute-done.35.refs_2_, ...), custom_call_target="tpu_custom_call" | custom-call | tf_op jit(solution)/shard_map/pallas_call | solution.py:182
  149.8 7.4 %collective-permute-done.25 = f32[96,256]{1,0:T(8,128)} collective-permute-done((f32[96,256]{1,0:T(8,128)S(1)}, f32[96,256]{1,0:T(8,128)}, u32[]{:S(2)}, u32[]{:S(2)}) %collective-permute-start.25) | collective-permute-done | bytes 98336 | tf_op jit(solution)/shard_map/ppermute | solution.py:377
  157.2 2.3 collective-permute-start.33
  161.3 2.1 collective-permute-start.43
  168.7 24.8 %collective-permute-done.33.refs_3_ = f32[2,384,256]{2,1,0:T(8,128)S(1)} collective-permute-done((f32[2,384,256]{2,1,0:T(8,128)}, f32[2,384,256]{2,1,0:T(8,128)S(1)}, u32[]{:S(2)}, u32[]{:S(2)}) %collective-permute-start.33) | collective-permute-done | bytes 786464 | tf_op jit(solution)/shard_map/ppermute | solution.py:377
  194.0 13.1 %collective-permute-done.42.refs_2_ = f32[384,512]{1,0:T(8,128)} collective-permute-done((f32[384,512]{1,0:T(8,128)}, f32[384,512]{1,0:T(8,128)}, u32[]{:S(2)}, u32[]{:S(2)}) %collective-permute-start.42) | collective-permute-done | bytes 786464 | tf_op jit(solution)/shard_map/ppermute | solution.py:377
  209.0 8.5 %shard_map.59 = (bf16[1536,512]{1,0:T(8,128)(2,1)}, bf16[1536,512]{1,0:T(8,128)(2,1)}, bf16[1536,512]{1,0:T(8,128)(2,1)}, bf16[1536,512]{1,0:T(8,128)(2,1)}, bf1...) custom-call(s32[1]{0:T(128)} %bitcast.8.slots_ref.row_ref, f32[2,256,256]{2,1,0:T(8,128)} %factors_ref.3, ...), custom_call_target="tpu_custom_call" | custom-call | tf_op jit(solution)/shard_map/pallas_call | solution.py:290
  220.4 12.2 %shard_map.60 = (bf16[1536,512]{1,0:T(8,128)(2,1)}, bf16[1536,512]{1,0:T(8,128)(2,1)}) custom-call(s32[1]{0:T(128)} %bitcast.8.slots_ref.row_ref, f32[2,256,256]{2,1,0:T(8,128)} %factors_ref.3, f32[256,256]{1,0:T(8,128)} %pad_maximum_fusion.11.c12_ref, f32[768,256]{1,0:T(8,128)} %pad_maximum_fusion.3.gram_ref, bf16[512,512]{1,0:T(8,128)(2,1)} %get-tuple-element.33.x_high, ...), custom_call_target="tpu_custom_call" | custom-call | tf_op jit(solution)/shard_map/pallas_call | solution.py:237
  232.6 23.0 %shard_map.61.matrix_ref = f32[3072,1536]{1,0:T(8,128)} custom-call(f32[3072,1536]{1,0:T(8,128)} %matrix_ref.5, f32[3072,512]{1,0:T(8,128)} %vectors_ref.5, bf16[1536,512]{1,0:T(8,128)(2,1)} %get-tuple-element.37.high_ref, bf16[1536,512]{1,0:T(8,128)(2,1)} %get-tuple-element.38.low_ref), custom_call_target="tpu_custom_call" | custom-call | tf_op jit(solution)/shard_map/pallas_call | solution.py:309
  255.5 14.6 %shard_map.63.matrix_ref = f32[3072,1536]{1,0:T(8,128)} custom-call(s32[4]{0:T(128)} %get-tuple-element.73.block_ref, f32[3072,1536]{1,0:T(8,128)} %shard_map.61.matrix_ref, bf16[1536,512]{1,0:T(8,128)(2,1)} %get-tuple-element.39.high_ref, bf16[1536,512]{1,0:T(8,128)(2,1)} %get-tuple-element.40.low_ref, ...), custom_call_target="tpu_custom_call", output_to_operand_aliasing={{}: (1, {})} | custom-call | tf_op jit(solution)/shard_map/pallas_call | solution.py:343
  270.2 14.4 %shard_map.64 = f32[3072,1536]{1,0:T(8,128)} custom-call(s32[4]{0:T(128)} %get-tuple-element.72.block_ref, f32[3072,1536]{1,0:T(8,128)} %shard_map.63.matrix_ref, bf16[1536,512]{1,0:T(8,128)(2,1)} %get-tuple-element.39.high_ref, bf16[1536,512]{1,0:T(8,128)(2,1)} %get-tuple-element.40.low_ref, ...), custom_call_target="tpu_custom_call", output_to_operand_aliasing={{}: (1, {})} | custom-call | tf_op jit(solution)/shard_map/pallas_call | solution.py:343
  (140 shorter events, 57.3 us)
Async XLA Ops:
  23.3 16.4 %collective-permute-start.8 = (f32[384,256]{1,0:T(8,128)}, f32[384,256]{1,0:T(8,128)S(1)}, u32[]{:S(2)}, u32[]{:S(2)}) collective-permute-start(f32[384,256]{1,0:T(8,128)} %get-tuple-element.32), channel_id=1, source_target_pairs={{0,16},{1,17},{2,18},{3,19},{4,20},{5,21},{6,22},{7,23},{8,24},{9,... | collective-permute-start | bytes 1179656 | tf_op jit(solution)/shard_map/ppermute | solution.py:377
  26.1 24.1 %collective-permute-start.12 = (f32[96,512]{1,0:T(8,128)S(1)}, f32[96,512]{1,0:T(8,128)S(1)}, u32[]{:S(2)}, u32[]{:S(2)}) collective-permute-start(f32[96,512]{1,0:T(8,128)S(1)} %get-tuple-element.48), channel_id=1, source_target_pairs={{0,24},{1,25},{2,26},{3,27},{4,28},{5,29},{6,30},{7,31},{8,16},{9,... | collective-permute-start | bytes 589832 | tf_op jit(solution)/shard_map/ppermute | solution.py:377
  26.1 24.7 %collective-permute-start.11 = (f32[96,512]{1,0:T(8,128)S(1)}, f32[96,512]{1,0:T(8,128)S(1)}, u32[]{:S(2)}, u32[]{:S(2)}) collective-permute-start(f32[96,512]{1,0:T(8,128)S(1)} %get-tuple-element.46), channel_id=1, source_target_pairs={{0,16},{1,17},{2,18},{3,19},{4,20},{5,21},{6,22},{7,23},{8,24},{9,... | collective-permute-start | bytes 589832 | tf_op jit(solution)/shard_map/ppermute | solution.py:377
  28.1 22.8 %collective-permute-start.10 = (f32[96,512]{1,0:T(8,128)S(1)}, f32[96,512]{1,0:T(8,128)S(1)}, u32[]{:S(2)}, u32[]{:S(2)}) collective-permute-start(f32[96,512]{1,0:T(8,128)S(1)} %get-tuple-element.47), channel_id=1, source_target_pairs={{0,8},{1,9},{2,10},{3,11},{4,12},{5,13},{6,14},{7,15},{8,0},{9,1},... | collective-permute-start | bytes 589832 | tf_op jit(solution)/shard_map/ppermute | solution.py:377
  33.5 21.2 %collective-permute-start.4 = (f32[384,256]{1,0:T(8,128)}, f32[384,256]{1,0:T(8,128)S(1)}, u32[]{:S(2)}, u32[]{:S(2)}) collective-permute-start(f32[384,256]{1,0:T(8,128)} %get-tuple-element.26), channel_id=1, source_target_pairs={{0,8},{1,9},{2,10},{3,11},{4,12},{5,13},{6,14},{7,15},{8,0},{9,1},... | collective-permute-start | bytes 1179656 | tf_op jit(solution)/shard_map/ppermute | solution.py:377
  39.7 15.0 %collective-permute-start.6 = (f32[384,256]{1,0:T(8,128)S(1)}, f32[384,256]{1,0:T(8,128)S(1)}, u32[]{:S(2)}, u32[]{:S(2)}) collective-permute-start(f32[384,256]{1,0:T(8,128)S(1)} %add.180), channel_id=1, source_target_pairs={{0,16},{1,17},{2,18},{3,19},{4,20},{5,21},{6,22},{7,23},{8,24},{9,... | collective-permute-start | bytes 1179656 | tf_op jit(solution)/shard_map/ppermute | solution.py:377
  51.0 19.2 %collective-permute-start.15 = (f32[96,512]{1,0:T(8,128)S(1)}, f32[96,512]{1,0:T(8,128)S(1)}, u32[]{:S(2)}, u32[]{:S(2)}) collective-permute-start(f32[96,512]{1,0:T(8,128)S(1)} %get-tuple-element.60), channel_id=1, source_target_pairs={{0,6},{1,7},{2,4},{3,5},{4,2},{5,3},{6,0},{7,1},{8,14},{9,15},{10,... | collective-permute-start | bytes 589832 | tf_op jit(solution)/shard_map/ppermute | solution.py:377
  54.7 17.1 %collective-permute-start.14 = (f32[96,512]{1,0:T(8,128)S(1)}, f32[96,512]{1,0:T(8,128)S(1)}, u32[]{:S(2)}, u32[]{:S(2)}) collective-permute-start(f32[96,512]{1,0:T(8,128)S(1)} %get-tuple-element.61), channel_id=1, source_target_pairs={{0,4},{1,5},{2,6},{3,7},{4,0},{5,1},{6,2},{7,3},{8,12},{9,13},{10,... | collective-permute-start | bytes 589832 | tf_op jit(solution)/shard_map/ppermute | solution.py:377
  54.7 17.6 %collective-permute-start.13 = (f32[96,512]{1,0:T(8,128)S(1)}, f32[96,512]{1,0:T(8,128)S(1)}, u32[]{:S(2)}, u32[]{:S(2)}) collective-permute-start(f32[96,512]{1,0:T(8,128)S(1)} %get-tuple-element.62), channel_id=1, source_target_pairs={{0,2},{1,3},{2,0},{3,1},{4,6},{5,7},{6,4},{7,5},{8,10},{9,11},{10,... | collective-permute-start | bytes 589832 | tf_op jit(solution)/shard_map/ppermute | solution.py:377
  60.6 19.2 %collective-permute-start.35 = (f32[384,512]{1,0:T(8,128)S(1)}, f32[384,512]{1,0:T(8,128)}, u32[]{:S(2)}, u32[]{:S(2)}) collective-permute-start(f32[384,512]{1,0:T(8,128)S(1)} %pad_maximum_fusion.6.refs_0_.refs_3_), channel_id=1, source_target_pairs={{0,2},{1,3},{2,4},{3,5},{4,6},{5,7},{8,10},{9,11},{10,12},{11,13},... | collective-permute-start | bytes 2359304 | tf_op jit(solution)/shard_map/ppermute | solution.py:377
  65.0 18.2 %collective-permute-start.38 = (f32[384,512]{1,0:T(8,128)S(1)}, f32[384,512]{1,0:T(8,128)}, u32[]{:S(2)}, u32[]{:S(2)}) collective-permute-start(f32[384,512]{1,0:T(8,128)S(1)} %pad_maximum_fusion.6.refs_0_.refs_3_), channel_id=1, source_target_pairs={{2,0},{3,1},{4,2},{5,3},{6,4},{7,5},{10,8},{11,9},{12,10},{13,11},... | collective-permute-start | bytes 2359304 | tf_op jit(solution)/shard_map/ppermute | solution.py:377
  79.7 30.2 %collective-permute-start.36 = (f32[384,512]{1,0:T(8,128)}, f32[384,512]{1,0:T(8,128)}, u32[]{:S(2)}, u32[]{:S(2)}) collective-permute-start(f32[384,512]{1,0:T(8,128)} %collective-permute-done.35.refs_2_), channel_id=1, source_target_pairs={{2,4},{3,5},{4,6},{5,7},{10,12},{11,13},{12,14},{13,15},{18,20},{1... | collective-permute-start | bytes 2359304 | tf_op jit(solution)/shard_map/ppermute | solution.py:377
  83.1 27.6 %collective-permute-start.39 = (f32[384,512]{1,0:T(8,128)}, f32[384,512]{1,0:T(8,128)}, u32[]{:S(2)}, u32[]{:S(2)}) collective-permute-start(f32[384,512]{1,0:T(8,128)} %collective-permute-done.38.refs_4_), channel_id=1, source_target_pairs={{2,0},{3,1},{4,2},{5,3},{10,8},{11,9},{12,10},{13,11},{18,16},{19,... | collective-permute-start | bytes 2359304 | tf_op jit(solution)/shard_map/ppermute | solution.py:377
  96.9 16.0 %collective-permute-start.28 = (f32[384,256]{1,0:T(8,128)}, f32[384,256]{1,0:T(8,128)S(1)}, u32[]{:S(2)}, u32[]{:S(2)}) collective-permute-start(f32[384,256]{1,0:T(8,128)} %get-tuple-element.51), channel_id=1, source_target_pairs={{0,16},{1,17},{2,18},{3,19},{4,20},{5,21},{6,22},{7,23},{8,24},{9,... | collective-permute-start | bytes 1179656 | tf_op jit(solution)/shard_map/ppermute | solution.py:377
  99.2 19.2 %collective-permute-start.31 = (f32[384,256]{1,0:T(8,128)S(1)}, f32[384,256]{1,0:T(8,128)S(1)}, u32[]{:S(2)}, u32[]{:S(2)}) collective-permute-start(f32[384,256]{1,0:T(8,128)S(1)} %copy-done.4), channel_id=1, source_target_pairs={{0,8},{1,9},{2,10},{3,11},{4,12},{5,13},{6,14},{7,15},{8,0},{9,1},... | collective-permute-start | bytes 1179656 | tf_op jit(solution)/shard_map/ppermute | solution.py:377
  108.5 52.8 %collective-permute-start.29 = (f32[2,384,256]{2,1,0:T(8,128)S(1)}, f32[2,384,256]{2,1,0:T(8,128)S(1)}, u32[]{:S(2)}, u32[]{:S(2)}) collective-permute-start(f32[2,384,256]{2,1,0:T(8,128)S(1)} %pad_maximum_fusion.4), channel_id=1, source_target_pairs={{0,16},{1,17},{2,18},{3,19},{4,20},{5,21},{6,22},{7,23},{8,24},{9,... | collective-permute-start | bytes 2359304 | tf_op jit(solution)/shard_map/ppermute | solution.py:377
  110.0 29.8 %collective-permute-start.37 = (f32[384,512]{1,0:T(8,128)}, f32[384,512]{1,0:T(8,128)S(1)}, u32[]{:S(2)}, u32[]{:S(2)}) collective-permute-start(f32[384,512]{1,0:T(8,128)} %collective-permute-done.36.refs_1_), channel_id=1, source_target_pairs={{4,6},{5,7},{12,14},{13,15},{20,22},{21,23},{28,30},{29,31}} | collective-permute-start | bytes 2359304 | tf_op jit(solution)/shard_map/ppermute | solution.py:377
  110.7 30.8 %collective-permute-start.40 = (f32[384,512]{1,0:T(8,128)}, f32[384,512]{1,0:T(8,128)S(1)}, u32[]{:S(2)}, u32[]{:S(2)}) collective-permute-start(f32[384,512]{1,0:T(8,128)} %collective-permute-done.39.refs_5_), channel_id=1, source_target_pairs={{2,0},{3,1},{10,8},{11,9},{18,16},{19,17},{26,24},{27,25}} | collective-permute-start | bytes 2359304 | tf_op jit(solution)/shard_map/ppermute | solution.py:377
  122.0 17.6 %collective-permute-start.32 = (f32[384,256]{1,0:T(8,128)S(1)}, f32[384,256]{1,0:T(8,128)S(1)}, u32[]{:S(2)}, u32[]{:S(2)}) collective-permute-start(f32[384,256]{1,0:T(8,128)S(1)} %copy-done.2), channel_id=1, source_target_pairs={{0,16},{1,17},{2,18},{3,19},{4,20},{5,21},{6,22},{7,23},{8,24},{9,... | collective-permute-start | bytes 1179656 | tf_op jit(solution)/shard_map/ppermute | solution.py:377
  137.3 27.3 %collective-permute-start.30 = (f32[2,384,256]{2,1,0:T(8,128)S(1)}, f32[2,384,256]{2,1,0:T(8,128)S(1)}, u32[]{:S(2)}, u32[]{:S(2)}) collective-permute-start(f32[2,384,256]{2,1,0:T(8,128)S(1)} %pad_maximum_fusion.5), channel_id=1, source_target_pairs={{0,8},{1,9},{2,10},{3,11},{4,12},{5,13},{6,14},{7,15},{8,0},{9,1},... | collective-permute-start | bytes 2359304 | tf_op jit(solution)/shard_map/ppermute | solution.py:377
  139.7 17.6 %collective-permute-start.25 = (f32[96,256]{1,0:T(8,128)S(1)}, f32[96,256]{1,0:T(8,128)}, u32[]{:S(2)}, u32[]{:S(2)}) collective-permute-start(f32[96,256]{1,0:T(8,128)S(1)} %add_add_fusion.3), channel_id=1, source_target_pairs={{0,24},{1,25},{2,26},{3,27},{4,28},{5,29},{6,30},{7,31},{8,16},{9,... | collective-permute-start | bytes 294920 | tf_op jit(solution)/shard_map/ppermute | solution.py:377
  139.8 19.8 %collective-permute-start.24 = (f32[96,256]{1,0:T(8,128)S(1)}, f32[96,256]{1,0:T(8,128)}, u32[]{:S(2)}, u32[]{:S(2)}) collective-permute-start(f32[96,256]{1,0:T(8,128)S(1)} %add_add_fusion.3), channel_id=1, source_target_pairs={{0,16},{1,17},{2,18},{3,19},{4,20},{5,21},{6,22},{7,23},{8,24},{9,... | collective-permute-start | bytes 294920 | tf_op jit(solution)/shard_map/ppermute | solution.py:377
  141.5 19.8 %collective-permute-start.23 = (f32[96,256]{1,0:T(8,128)S(1)}, f32[96,256]{1,0:T(8,128)}, u32[]{:S(2)}, u32[]{:S(2)}) collective-permute-start(f32[96,256]{1,0:T(8,128)S(1)} %add_add_fusion.3), channel_id=1, source_target_pairs={{0,8},{1,9},{2,10},{3,11},{4,12},{5,13},{6,14},{7,15},{8,0},{9,1},... | collective-permute-start | bytes 294920 | tf_op jit(solution)/shard_map/ppermute | solution.py:377
  157.2 36.2 %collective-permute-start.33 = (f32[2,384,256]{2,1,0:T(8,128)}, f32[2,384,256]{2,1,0:T(8,128)S(1)}, u32[]{:S(2)}, u32[]{:S(2)}) collective-permute-start(f32[2,384,256]{2,1,0:T(8,128)} %pad_maximum_fusion.7), channel_id=1, source_target_pairs={{0,16},{1,17},{2,18},{3,19},{4,20},{5,21},{6,22},{7,23},{8,24},{9,... | collective-permute-start | bytes 2359304 | tf_op jit(solution)/shard_map/ppermute | solution.py:377
  159.5 33.9 %collective-permute-start.41 = (f32[384,512]{1,0:T(8,128)}, f32[384,512]{1,0:T(8,128)}, u32[]{:S(2)}, u32[]{:S(2)}) collective-permute-start(f32[384,512]{1,0:T(8,128)} %get-tuple-element.42), channel_id=1, source_target_pairs={{0,8},{1,9},{2,10},{3,11},{4,12},{5,13},{6,14},{7,15},{8,0},{9,1},... | collective-permute-start | bytes 2359304 | tf_op jit(solution)/shard_map/ppermute | solution.py:377
  161.3 45.8 %collective-permute-start.42 = (f32[384,512]{1,0:T(8,128)}, f32[384,512]{1,0:T(8,128)}, u32[]{:S(2)}, u32[]{:S(2)}) collective-permute-start(f32[384,512]{1,0:T(8,128)} %get-tuple-element.43), channel_id=1, source_target_pairs={{0,16},{1,17},{2,18},{3,19},{4,20},{5,21},{6,22},{7,23},{8,24},{9,... | collective-permute-start | bytes 2359304 | tf_op jit(solution)/shard_map/ppermute | solution.py:377
  161.3 45.8 %collective-permute-start.43 = (f32[384,512]{1,0:T(8,128)}, f32[384,512]{1,0:T(8,128)}, u32[]{:S(2)}, u32[]{:S(2)}) collective-permute-start(f32[384,512]{1,0:T(8,128)} %get-tuple-element.44), channel_id=1, source_target_pairs={{0,24},{1,25},{2,26},{3,27},{4,28},{5,29},{6,30},{7,31},{8,16},{9,... | collective-permute-start | bytes 2359304 | tf_op jit(solution)/shard_map/ppermute | solution.py:377
  167.3 52.2 %collective-permute-start.34 = (f32[2,384,256]{2,1,0:T(8,128)}, f32[2,384,256]{2,1,0:T(8,128)S(1)}, u32[]{:S(2)}, u32[]{:S(2)}) collective-permute-start(f32[2,384,256]{2,1,0:T(8,128)} %pad_maximum_fusion.8), channel_id=1, source_target_pairs={{0,8},{1,9},{2,10},{3,11},{4,12},{5,13},{6,14},{7,15},{8,0},{9,1},... | collective-permute-start | bytes 2359304 | tf_op jit(solution)/shard_map/ppermute | solution.py:377
  193.5 76.6 %collective-permute-start.44 = (f32[384,512]{1,0:T(8,128)}, f32[384,512]{1,0:T(8,128)}, u32[]{:S(2)}, u32[]{:S(2)}) collective-permute-start(f32[384,512]{1,0:T(8,128)} %get-tuple-element.41.refs_0_), channel_id=1, source_target_pairs={{0,1},{1,0},{2,3},{3,2},{4,5},{5,4},{6,7},{7,6},{8,9},{9,8},{10,11... | collective-permute-start | bytes 2359304 | tf_op jit(solution)/shard_map/ppermute | solution.py:377
  193.5 76.6 %collective-permute-start.45 = (f32[384,512]{1,0:T(8,128)}, f32[384,512]{1,0:T(8,128)}, u32[]{:S(2)}, u32[]{:S(2)}) collective-permute-start(f32[384,512]{1,0:T(8,128)} %collective-permute-done.41.refs_1_), channel_id=1, source_target_pairs={{0,1},{1,0},{2,3},{3,2},{4,5},{5,4},{6,7},{7,6},{8,9},{9,8},{10,11... | collective-permute-start | bytes 2359304 | tf_op jit(solution)/shard_map/ppermute | solution.py:377
  207.1 63.0 %collective-permute-start.46 = (f32[384,512]{1,0:T(8,128)}, f32[384,512]{1,0:T(8,128)}, u32[]{:S(2)}, u32[]{:S(2)}) collective-permute-start(f32[384,512]{1,0:T(8,128)} %collective-permute-done.42.refs_2_), channel_id=1, source_target_pairs={{0,1},{1,0},{2,3},{3,2},{4,5},{5,4},{6,7},{7,6},{8,9},{9,8},{10,11... | collective-permute-start | bytes 2359304 | tf_op jit(solution)/shard_map/ppermute | solution.py:377
  207.1 63.0 %collective-permute-start.47 = (f32[384,512]{1,0:T(8,128)}, f32[384,512]{1,0:T(8,128)}, u32[]{:S(2)}, u32[]{:S(2)}) collective-permute-start(f32[384,512]{1,0:T(8,128)} %collective-permute-done.43.refs_3_), channel_id=1, source_target_pairs={{0,1},{1,0},{2,3},{3,2},{4,5},{5,4},{6,7},{7,6},{8,9},{9,8},{10,11... | collective-permute-start | bytes 2359304 | tf_op jit(solution)/shard_map/ppermute | solution.py:377
  (33 other events, 550.7 us)
